TPU v7x, 512 devices: a whole 4x8x8 slice. The times are simulated.
512 devices in a mesh: dp: 8 (over x, core), ctx: 64 (over y, z).
Axes of the slice: x: 4, y: 8, z: 8, core: 2. Of those that a mesh axis runs over, the one named last changes fastest.
Arguments:
- queries: bfloat16 [8192, 4096], P(('dp', 'ctx')), may hold values from -150 to 150
- keys: bfloat16 [131072, 1024], P(('dp', 'ctx')), may hold values from -8 to 8
- values: bfloat16 [131072, 1024], P(('dp', 'ctx')), may hold values from -6 to 6
- learned_compress_queries: bfloat16 [16, 1024], replicated, may hold values from -150 to 150
- span_len: int32 [8, 64], P('dp', 'ctx'), may hold values from 1 to 16, 768 in all within a row
- span_offset: int32 [8, 64], P('dp', 'ctx'), may hold values from 0 to 240
- destination: int32 [8192, 1], P(('dp', 'ctx')), may hold values from 0 to 63; in each aligned block of 16 rows (0 to 15, 16 to 31, ...) at most 2 rows name the same one
- cotangent: bfloat16 [8192, 4096], P(('dp', 'ctx')), may hold values from -6 to 6
- adapter_a: bfloat16 [64, 16, 4096], P('ctx'), may hold values from -0.09375 to 0.09375
- adapter_b: bfloat16 [64, 16, 4096], P('ctx'), may hold values from -0.09375 to 0.09375
Outputs:
- grad_rows: bfloat16 [8192, 4096], P(('dp', 'ctx'))
- grad_a: float32 [64, 16, 4096], P('ctx')
- grad_b: float32 [64, 16, 4096], P('ctx')
Inputs may be any that keep to these rules, and one draw needn't show every extreme that they name: `destination`: in each device's 16 slots (aligned blocks of rows) no decoder is named more than 2 times, a bound that some block reaches.
All inputs are finite; a program needn't handle non-finite values. No bound on the sum of `span_len` on one device may be relied on, other than what follows from the above.
Results may differ from a plain program's by a relative error of at most 0.025.
Values may be sent and summed in bfloat16 or wider, within the bound.
A program may use at most 64 MiB of HBM per device.

v0:
```python
import math
import jax
import jax.numpy as jnp
from jax import lax
from jax.sharding import PartitionSpec as P

QUERY_HEADS = 32
KEY_VALUE_HEADS = 8
HEAD_SIZE = 128
COMPRESSED_ROWS = 16
SCALE = 2.0
EPS = 1e-06
NEGATIVE_FLOOR = -1e30


def absorb(state, query_matrix, keys_blk, vals_blk, visible):
    count = keys_blk.shape[0]
    heads = query_matrix.shape[1]
    width = query_matrix.shape[3]
    expanded_keys = keys_blk.reshape(count, heads, width)
    expanded_values = vals_blk.reshape(count, heads, width)
    attention_score = jnp.einsum(
        "shgd,nhd->shgn", query_matrix, expanded_keys, preferred_element_type=jnp.float32
    ) * (1.0 / math.sqrt(width))
    seen = visible[:, None, None, :]
    attention_score = jnp.where(seen, attention_score, NEGATIVE_FLOOR)
    peak, total, accum = state
    newpeak = jnp.maximum(peak, jnp.max(attention_score, axis=-1))
    keep = jnp.exp(peak - newpeak)
    prob = jnp.where(seen, jnp.exp(attention_score - newpeak[..., None]), 0.0)
    total = total * keep + jnp.sum(prob, axis=-1)
    accum = accum * keep[..., None] + jnp.einsum(
        "shgn,nhd->shgd",
        prob.astype(jnp.bfloat16),
        expanded_values,
        preferred_element_type=jnp.float32,
    )
    return (newpeak, total, accum)


def absorb_rows(state, query_matrix, keys_blk, vals_blk, visible):
    count = keys_blk.shape[0]
    blocks = count // 256
    kb = keys_blk.reshape(blocks, 256, keys_blk.shape[1])
    vb = vals_blk.reshape(blocks, 256, vals_blk.shape[1])
    mb = visible.reshape(visible.shape[0], blocks, 256).transpose(1, 0, 2)

    def step(current, item):
        return (absorb(current, query_matrix, item[0], item[1], item[2]), None)

    state, _ = lax.scan(step, state, (kb, vb, mb))
    return state


def attend(queries, keys, values, learned_compress_queries, offset, length):
    span_slots = queries.shape[0]
    model = queries.shape[1]
    segment_length = keys.shape[0]
    query_group = QUERY_HEADS // KEY_VALUE_HEADS
    here = lax.axis_index("ctx")
    query_matrix = queries.reshape(span_slots, KEY_VALUE_HEADS, query_group, HEAD_SIZE)
    expanded_keys = keys.reshape(segment_length, KEY_VALUE_HEADS, HEAD_SIZE)
    expanded_values = values.reshape(segment_length, KEY_VALUE_HEADS, HEAD_SIZE)
    compressor_query = learned_compress_queries.reshape(COMPRESSED_ROWS, KEY_VALUE_HEADS, HEAD_SIZE)
    attention_score = jnp.einsum(
        "cpf,ipf->pci", compressor_query, expanded_keys, preferred_element_type=jnp.float32
    ) * (1.0 / math.sqrt(HEAD_SIZE))
    softmax_weight = jax.nn.softmax(attention_score, axis=-1).astype(jnp.bfloat16)
    short_keys = (
        jnp.einsum(
            "wio,owx->iwx", softmax_weight, expanded_keys, preferred_element_type=jnp.float32
        )
        .astype(jnp.bfloat16)
        .reshape(COMPRESSED_ROWS, KEY_VALUE_HEADS * HEAD_SIZE)
    )
    short_vals = (
        jnp.einsum(
            "wio,owx->iwx", softmax_weight, expanded_values, preferred_element_type=jnp.float32
        )
        .astype(jnp.bfloat16)
        .reshape(COMPRESSED_ROWS, KEY_VALUE_HEADS * HEAD_SIZE)
    )
    state = (
        jnp.full((span_slots, KEY_VALUE_HEADS, query_group), NEGATIVE_FLOOR, jnp.float32),
        jnp.zeros((span_slots, KEY_VALUE_HEADS, query_group), jnp.float32),
        jnp.zeros((span_slots, KEY_VALUE_HEADS, query_group, HEAD_SIZE), jnp.float32),
    )
    position = offset + jnp.arange(span_slots, dtype=jnp.int32)
    local = jnp.arange(segment_length, dtype=jnp.int32)[None, :] <= position[:, None]
    state = absorb(state, query_matrix, keys, values, local)
    piece = (
        lax.all_gather(short_keys, "ctx", axis=0, tiled=True),
        lax.all_gather(short_vals, "ctx", axis=0, tiled=True),
    )
    count = piece[0].shape[0]
    source = jnp.arange(count, dtype=jnp.int32) // COMPRESSED_ROWS
    state = absorb_rows(state, query_matrix, piece[0], piece[1], (source < here)[None, :])
    peak, total, accum = state
    out = (accum / total[..., None]).reshape(span_slots, model)
    live = (jnp.arange(span_slots, dtype=jnp.int32) < length)[:, None]
    return jnp.where(live, out, 0.0).astype(jnp.bfloat16)


def shards(
    queries,
    keys,
    values,
    learned_compress_queries,
    span_len,
    span_offset,
    destination,
    cotangent,
    adapter_a,
    adapter_b,
):
    span_slots = queries.shape[0]
    model = queries.shape[1]
    count = lax.axis_size("ctx")
    cap = max(2, (3 * span_slots + 2 * count - 1) // (2 * count))
    offset = span_offset[0, 0]
    length = span_len[0, 0]
    live = (jnp.arange(span_slots, dtype=jnp.int32) < length)[:, None]
    dy = jnp.where(live, cotangent, jnp.zeros_like(cotangent))
    target = destination[:, 0]
    order_idx = jnp.arange(span_slots, dtype=jnp.int32)
    same = target[:, None] == target[None, :]
    before = order_idx[None, :] < order_idx[:, None]
    rank = jnp.sum((same & before).astype(jnp.int32), axis=1)
    slot = target * cap + rank
    place = (jnp.arange(count * cap, dtype=jnp.int32)[:, None] == slot[None, :]).astype(
        jnp.bfloat16
    )

    def packed(row_block):
        return (
            jnp.dot(place, row_block, preferred_element_type=jnp.float32)
            .astype(jnp.bfloat16)
            .reshape(count, cap, model)
        )

    attn = attend(queries, keys, values, learned_compress_queries, offset, length)
    rows_in, dy_in = (
        lax.all_to_all(packed(attn), "ctx", split_axis=0, concat_axis=0, tiled=True),
        lax.all_to_all(packed(dy), "ctx", split_axis=0, concat_axis=0, tiled=True),
    )
    x = rows_in.reshape(count * cap, model).astype(jnp.float32)
    grads_in = dy_in.reshape(count * cap, model)
    rs = lax.rsqrt(jnp.mean(x * x, axis=-1, keepdims=True) + EPS)
    nrm = x * rs
    normed = nrm.astype(jnp.bfloat16)
    down = adapter_a[0]
    upper = adapter_b[0]
    across = (((1,), (1,)), ((), ()))
    along = (((0,), (0,)), ((), ()))
    hid = lax.dot_general(normed, down, across, preferred_element_type=jnp.float32).astype(
        jnp.bfloat16
    )
    back = (
        SCALE * lax.dot_general(grads_in, upper, across, preferred_element_type=jnp.float32)
    ).astype(jnp.bfloat16)
    grad_b = SCALE * lax.dot_general(hid, grads_in, along, preferred_element_type=jnp.float32)
    grad_a = lax.dot_general(back, normed, along, preferred_element_type=jnp.float32)
    dn = jnp.dot(back, down, preferred_element_type=jnp.float32)
    d_rows = (
        grads_in.astype(jnp.float32) + rs * (dn - nrm * jnp.mean(dn * nrm, axis=-1, keepdims=True))
    ).astype(jnp.bfloat16)
    returned = lax.all_to_all(
        d_rows.reshape(count, cap, model), "ctx", split_axis=0, concat_axis=0, tiled=True
    )
    grad_rows = lax.dot_general(
        place, returned.reshape(count * cap, model), along, preferred_element_type=jnp.float32
    ).astype(jnp.bfloat16)
    grad_a, grad_b = (
        lax.psum(grad_a.astype(jnp.bfloat16), "dp").astype(jnp.float32),
        lax.psum(grad_b.astype(jnp.bfloat16), "dp").astype(jnp.float32),
    )
    return (grad_rows, grad_a[None], grad_b[None])


def solution(mesh):
    in_specs = (
        P(("dp", "ctx"), None),
        P(("dp", "ctx"), None),
        P(("dp", "ctx"), None),
        P(),
        P("dp", "ctx"),
        P("dp", "ctx"),
        P(("dp", "ctx"), None),
        P(("dp", "ctx"), None),
        P("ctx", None, None),
        P("ctx", None, None),
    )
    out_specs = (P(("dp", "ctx"), None), P("ctx", None, None), P("ctx", None, None))
    return jax.shard_map(shards, mesh=mesh, in_specs=in_specs, out_specs=out_specs, check_vma=False)
```

profile of v0, /device:TPU:8, one launch (start us, length us, event | category | flops | bytes accessed | tf_op | source)
XLA Modules:
  0.0 355.6 jit_solution(18318135870249494899)
XLA Ops:
  7.2 1.5 fusion.61
  8.8 1.3 fusion.19
  10.8 1.3 fusion.20
  14.1 1.5 reshape.203
  15.6 16.9 %all-to-all-start = ((bf16[64,2,4096]{2,1,0:T(2,128)(2,1)}), bf16[64,2,4096]{2,1,0:T(2,128)(2,1)}, u32[]{:S(2)}, u32[]{:S(2)}) async-start(bf16[64,2,4096]{2,1,0:T(2,128)(2,1)} %reshape.203), calls=%async_computation | async-start | bytes 2097152 | tf_op jit(solution)/shard_map/all_to_all | solution.py:144
  34.6 82.2 %all-gather.3.cloned.1.call-done = bf16[1024,1024]{1,0:T(8,128)(2,1)} async-done(((bf16[16,1024]{1,0:T(8,128)(2,1)}), bf16[1024,1024]{1,0:T(8,128)(2,1)}) %all-gather.3.cloned.1.call-update) | async-done | bytes 2097168 | tf_op jit(solution)/shard_map/all_gather | solution.py:92
  116.9 84.1 %all-gather.5.cloned.1.call-done = bf16[1024,1024]{1,0:T(8,128)(2,1)} async-done(((bf16[16,1024]{1,0:T(8,128)(2,1)}), bf16[1024,1024]{1,0:T(8,128)(2,1)}) %all-gather.5.cloned.1.call-update) | async-done | bytes 2097168 | tf_op jit(solution)/shard_map/all_gather | solution.py:93
  201.0 11.0 %while.14 = (s32[]{:T(128)}, f32[16,8,4]{0,2,1:T(4,128)S(1)}, f32[16,8,4]{0,2,1:T(4,128)S(1)}, f32[16,8,4,128]{3,0,2,1:T(8,128)S(1)}, pred[4,1,256]{2,1,0:T(4,12...) while((s32[]{:T(128)}, f32[16,8,4]{0,2,1:T(4,128)S(1)}, ...), condition=%wide.region_8.9_spmd, body=%wide.region_5.8_spmd.sunk | while | flops 68420608 | bytes 7505253 | solution.py:51
  203.8 1.3 constant_dynamic-slice_fusion.3
  206.5 1.3 constant_dynamic-slice_fusion.3
  212.8 1.5 reshape.214
  214.3 9.5 %all-to-all-start.1 = ((bf16[64,2,4096]{2,1,0:T(2,128)(2,1)}), bf16[64,2,4096]{2,1,0:T(2,128)(2,1)S(1)}, u32[]{:S(2)}, u32[]{:S(2)}) async-start(bf16[64,2,4096]{2,1,0:T(2,128)(2,1)} %reshape.214), calls=%async_computation.1 | async-start | bytes 2097152 | tf_op jit(solution)/shard_map/all_to_all | solution.py:143
  223.8 1.5 reshape.204
  225.7 23.5 %all-to-all-done.1 = bf16[64,2,4096]{2,1,0:T(2,128)(2,1)S(1)} async-done(((bf16[64,2,4096]{2,1,0:T(2,128)(2,1)}), bf16[64,2,4096]{2,1,0:T(2,128)(2,1)S(1)}, u32[]{:S(2)}, u32[]{:S(2)}) %all-to-all-start.1) | async-done | bytes 1048608 | tf_op jit(solution)/shard_map/all_to_all | solution.py:143
  252.1 1.7 add_convert_fusion
  253.8 2.5 reshape.215
  256.3 6.9 %all-to-all-start.2 = ((bf16[64,2,4096]{2,1,0:T(2,128)(2,1)}), bf16[64,2,4096]{2,1,0:T(2,128)(2,1)}, u32[]{:S(2)}, u32[]{:S(2)}) async-start(bf16[64,2,4096]{2,1,0:T(2,128)(2,1)} %reshape.215), calls=%async_computation.2 | async-start | bytes 2097152 | tf_op jit(solution)/shard_map/all_to_all | solution.py:167
  263.4 2.4 multiply_convert_fusion
  265.8 2.3 convert_element_type.95
  269.1 2.8 fusion.13
  271.9 71.4 %all-reduce.3.cloned.1.call-done = (bf16[1,16,4096]{2,1,0:T(8,128)(2,1)}, bf16[1,16,4096]{2,1,0:T(8,128)(2,1)}) async-done(((bf16[1,16,4096]{2,1,0:T(8,128)(2,1)}, bf16[1,16,4096]{2,1,0:T(8,128)(2,1)}), (bf16[1,16,4096]{2,1,0:T(8,128)(2,1)}, bf16[1,16,4096]{2,1,0:T(8,128)(2,1)})) %all-reduce.3.cloned.1.call-update) | async-done | bytes 262160 | tf_op jit(solution)/shard_map/psum | solution.py:174
  343.4 1.6 broadcast_in_dim.108
  345.0 1.6 broadcast_in_dim.110
  346.6 1.5 reshape.216
  (97 shorter events, 17.9 us)
Async XLA Ops:
  7.2 243.7 %copy-start = (bf16[1,16,4096]{2,1,0:T(8,128)(2,1)S(1)}, bf16[1,16,4096]{2,1,0:T(8,128)(2,1)}, u32[]{:S(2)}) copy-start(bf16[1,16,4096]{2,1,0:T(8,128)(2,1)} %param.20) | copy-start | bytes 393220
  7.2 6.2 %copy-start.9 = (s32[16,1]{0,1:T(1,128)S(1)}, s32[16,1]{0,1:T(1,128)}, u32[]{:S(2)}) copy-start(s32[16,1]{0,1:T(1,128)} %param.18) | copy-start | bytes 196
  7.2 6.4 %copy-start.8 = (bf16[16,4096]{1,0:T(8,128)(2,1)S(1)}, bf16[16,4096]{1,0:T(8,128)(2,1)}, u32[]{:S(2)}) copy-start(bf16[16,4096]{1,0:T(8,128)(2,1)} %param.19) | copy-start | bytes 393220
  7.2 109.7 %all-gather.3.cloned.1.call-start = ((), (), s32[]{:S(2)}) async-start(), calls=%async_computation.3 | async-start | bytes 2129920 | tf_op jit(solution)/shard_map/all_gather | solution.py:92
  10.7 190.3 %all-gather.5.cloned.1.call-start = ((), (), s32[]{:S(2)}) async-start(), calls=%async_computation.4 | async-start | bytes 2129920 | tf_op jit(solution)/shard_map/all_gather | solution.py:93
  14.0 19.1 %copy-start.7 = (bf16[16,4096]{1,0:T(8,128)(2,1)S(1)}, bf16[16,4096]{1,0:T(8,128)(2,1)}, u32[]{:S(2)}) copy-start(bf16[16,4096]{1,0:T(8,128)(2,1)} %param.12) | copy-start | bytes 393220
  14.1 19.2 %copy-start.4 = (bf16[256,1024]{1,0:T(8,128)(2,1)S(1)}, bf16[256,1024]{1,0:T(8,128)(2,1)}, u32[]{:S(2)}) copy-start(bf16[256,1024]{1,0:T(8,128)(2,1)} %param.13) | copy-start | bytes 1572868
  15.6 17.8 %copy-start.5 = (bf16[256,1024]{1,0:T(8,128)(2,1)S(1)}, bf16[256,1024]{1,0:T(8,128)(2,1)}, u32[]{:S(2)}) copy-start(bf16[256,1024]{1,0:T(8,128)(2,1)} %param.14) | copy-start | bytes 1572868
  15.6 198.7 %all-to-all-start = ((bf16[64,2,4096]{2,1,0:T(2,128)(2,1)}), bf16[64,2,4096]{2,1,0:T(2,128)(2,1)}, u32[]{:S(2)}, u32[]{:S(2)}) async-start(bf16[64,2,4096]{2,1,0:T(2,128)(2,1)} %reshape.203), calls=%async_computation | async-start | bytes 2097152 | tf_op jit(solution)/shard_map/all_to_all | solution.py:144
  214.3 11.0 %copy-start.6 = (bf16[1,16,4096]{2,1,0:T(8,128)(2,1)S(1)}, bf16[1,16,4096]{2,1,0:T(8,128)(2,1)}, u32[]{:S(2)}) copy-start(bf16[1,16,4096]{2,1,0:T(8,128)(2,1)} %param.21) | copy-start | bytes 393220
  214.3 34.9 %all-to-all-start.1 = ((bf16[64,2,4096]{2,1,0:T(2,128)(2,1)}), bf16[64,2,4096]{2,1,0:T(2,128)(2,1)S(1)}, u32[]{:S(2)}, u32[]{:S(2)}) async-start(bf16[64,2,4096]{2,1,0:T(2,128)(2,1)} %reshape.214), calls=%async_computation.1 | async-start | bytes 2097152 | tf_op jit(solution)/shard_map/all_to_all | solution.py:143
  225.3 25.1 %copy-start.1 = (bf16[128,4096]{1,0:T(8,128)(2,1)}, bf16[128,4096]{1,0:T(8,128)(2,1)S(1)}, u32[]{:S(2)}) copy-start(bf16[128,4096]{1,0:T(8,128)(2,1)S(1)} %reshape.204) | copy-start | bytes 3145732
  250.9 1.2 copy-start.2
  256.3 90.3 %all-to-all-start.2 = ((bf16[64,2,4096]{2,1,0:T(2,128)(2,1)}), bf16[64,2,4096]{2,1,0:T(2,128)(2,1)}, u32[]{:S(2)}, u32[]{:S(2)}) async-start(bf16[64,2,4096]{2,1,0:T(2,128)(2,1)} %reshape.215), calls=%async_computation.2 | async-start | bytes 2097152 | tf_op jit(solution)/shard_map/all_to_all | solution.py:167
  263.2 80.2 %all-reduce.3.cloned.1.call-start = ((), (), s32[]{:S(2)}) async-start(), calls=%async_computation.5 | async-start | bytes 524288 | tf_op jit(solution)/shard_map/psum | solution.py:174
  265.8 3.3 copy-start.3
Sparse Core Ops, SparseCore 0:
  11.6 105.2 all-gather.2
  120.5 80.5 all-gather.4
  272.1 71.2 all-reduce.2
where the time goes:
time: 356 us
  waiting for transfers between devices  261 us (73%)
  starting transfers between devices  33.6 us (9%)
  local copies, waits for them, and re-layouts  20.5 us (6%)
  between operations  15.3 us (4%)
  matrix products  14.1 us (4%)
  other arithmetic  10.5 us (3%)
    all_gather x1, waiting for transfers between devices, attend(): lax.all_gather(short_vals, 'ctx', axis=0, tiled=True)  84.1 us
    all_gather x1, waiting for transfers between devices, attend(): lax.all_gather(short_keys, 'ctx', axis=0, tiled=True)  82.2 us
    psum x1, waiting for transfers between devices, shards(): lax.psum(grad_a.astype(jnp.bfloat16), 'dp').astype(jnp.float32)  71.4 us
    all_to_all x1, waiting for transfers between devices, shards(): lax.all_to_all(packed(attn), 'ctx', split_axis=0, concat_axis=0, tiled=True)  23.5 us
    all_to_all x1, starting transfers between devices, shards(): lax.all_to_all(packed(dy), 'ctx', split_axis=0, concat_axis=0, tiled=True)  16.9 us
    all_to_all x1, starting transfers between devices, shards(): lax.all_to_all(packed(attn), 'ctx', split_axis=0, concat_axis=0, tiled=True)  9.51 us
  transfers between devices with their start and end apart: 6, of which 4 were waited for; matrix products, arithmetic and copies ran while one was open for 9% of the time, Pallas kernels for 0%

commit v1 on v0

--- a/solution.py
+++ b/solution.py
@@ -11,6 +11,13 @@
 SCALE = 2.0
 EPS = 1e-06
 NEGATIVE_FLOOR = -1e30
+
+
+def gather_over(x, axis, along):
+    peers = lax.axis_size(axis)
+    blocks = jnp.stack([x for _ in range(peers)])
+    blocks = lax.all_to_all(blocks, axis, split_axis=0, concat_axis=0)
+    return jnp.concatenate(blocks, axis=along)
 
 
 def absorb(state, query_matrix, keys_blk, vals_blk, visible):
@@ -89,7 +96,7 @@
     local = jnp.arange(segment_length, dtype=jnp.int32)[None, :] <= position[:, None]
     state = absorb(state, query_matrix, keys, values, local)
     piece = (
-        lax.all_gather(short_keys, "ctx", axis=0, tiled=True),
+        gather_over(short_keys, "ctx", 0),
         lax.all_gather(short_vals, "ctx", axis=0, tiled=True),
     )
     count = piece[0].shape[0]

time: 356 us -> 311 us (0.87)
  waiting for transfers between devices: 261 us -> 207 us
  starting transfers between devices: 33.6 us -> 43 us
    all_gather x1 -> x0, waiting for transfers between devices: 82.2 us -> none  [attend(): lax.all_gather(short_keys, 'ctx', axis=0, tiled=True)]
    all_to_all x0 -> x1, waiting for transfers between devices: none -> 46.4 us  [gather_over(): blocks = lax.all_to_all(blocks, axis, split_axis=0, concat_axis=0)]
    all_gather x1, waiting for transfers between devices: 84.1 us -> 64.7 us  [attend(): lax.all_gather(short_vals, 'ctx', axis=0, tiled=True)]
    all_to_all x0 -> x1, starting transfers between devices: none -> 16.9 us  [gather_over(): blocks = lax.all_to_all(blocks, axis, split_axis=0, concat_axis=0)]
    all_to_all x1, starting transfers between devices: 16.9 us -> 9.68 us  [shards(): lax.all_to_all(packed(dy), 'ctx', split_axis=0, concat_axis=0, tiled=True)]
  transfers between devices with their start and end apart: 6 -> 6, of which waited for: 4 -> 4; matrix products, arithmetic and copies ran while one was open for 9% -> 10% of each run, Pallas kernels for 0% -> 0%
where the time goes in v1:
time: 311 us; the launch traced here: 310 us
  waiting for transfers between devices  207 us (67%)
  starting transfers between devices  43 us (14%)
  local copies, waits for them, and re-layouts  20.5 us (7%)
  between operations  15.6 us (5%)
  matrix products  13 us (4%)
  other arithmetic  10.5 us (3%)
    psum x1, waiting for transfers between devices, shards(): lax.psum(grad_a.astype(jnp.bfloat16), 'dp').astype(jnp.float32)  71.4 us
    all_gather x1, waiting for transfers between devices, attend(): lax.all_gather(short_vals, 'ctx', axis=0, tiled=True)  64.7 us
    all_to_all x1, waiting for transfers between devices, gather_over(): blocks = lax.all_to_all(blocks, axis, split_axis=0, concat_axis=0)  46.4 us
    all_to_all x1, waiting for transfers between devices, shards(): lax.all_to_all(packed(attn), 'ctx', split_axis=0, concat_axis=0, tiled=True)  24.5 us
    all_to_all x1, starting transfers between devices, gather_over(): blocks = lax.all_to_all(blocks, axis, split_axis=0, concat_axis=0)  16.9 us
    all_to_all x1, starting transfers between devices, shards(): lax.all_to_all(packed(dy), 'ctx', split_axis=0, concat_axis=0, tiled=True)  9.68 us
    all_to_all x1, starting transfers between devices, shards(): lax.all_to_all(packed(attn), 'ctx', split_axis=0, concat_axis=0, tiled=True)  9.51 us
    all_to_all x1, starting transfers between devices, shards(): lax.all_to_all(d_rows.reshape(count, cap, model), 'ctx', split_axis=0, co...  6.85 us
  transfers between devices with their start and end apart: 6, of which 4 were waited for; matrix products, arithmetic and copies ran while one was open for 10% of the time, Pallas kernels for 0%

profile of v1, /device:TPU:8, one launch (start us, length us, event | category | flops | bytes accessed | tf_op | source)
XLA Modules:
  0.0 309.8 jit_solution(9793872628496878645)
XLA Ops:
  7.2 1.5 fusion.61
  8.7 1.3 fusion.19
  10.0 1.6 stack.3
  11.6 16.9 %all-to-all-start.1 = ((bf16[64,16,1024]{2,1,0:T(8,128)(2,1)}), bf16[64,16,1024]{2,1,0:T(8,128)(2,1)}, u32[]{:S(2)}, u32[]{:S(2)}) async-start(bf16[64,16,1024]{2,1,0:T(8,128)(2,1)} %stack.3), calls=%async_computation.1 | async-start | bytes 4194304 | tf_op jit(solution)/shard_map/all_to_all | solution.py:19
  31.8 1.5 reshape.199
  34.5 46.4 %all-to-all-done.1 = bf16[64,16,1024]{2,1,0:T(8,128)(2,1)} async-done(((bf16[64,16,1024]{2,1,0:T(8,128)(2,1)}), bf16[64,16,1024]{2,1,0:T(8,128)(2,1)}, u32[]{:S(2)}, u32[]{:S(2)}) %all-to-all-start.1) | async-done | bytes 2097184 | tf_op jit(solution)/shard_map/all_to_all | solution.py:19
  80.8 9.7 %all-to-all-start = ((bf16[64,2,4096]{2,1,0:T(2,128)(2,1)}), bf16[64,2,4096]{2,1,0:T(2,128)(2,1)S(1)}, u32[]{:S(2)}, u32[]{:S(2)}) async-start(bf16[64,2,4096]{2,1,0:T(2,128)(2,1)} %reshape.199), calls=%async_computation | async-start | bytes 2097152 | tf_op jit(solution)/shard_map/all_to_all | solution.py:151
  90.5 64.7 %all-gather.2.cloned.1.call-done = bf16[1024,1024]{1,0:T(8,128)(2,1)} async-done(((bf16[16,1024]{1,0:T(8,128)(2,1)}), bf16[1024,1024]{1,0:T(8,128)(2,1)}) %all-gather.2.cloned.1.call-update) | async-done | bytes 2097168 | tf_op jit(solution)/shard_map/all_gather | solution.py:100
  155.2 11.0 %while.14 = (s32[]{:T(128)}, f32[16,8,4]{0,2,1:T(4,128)S(1)}, f32[16,8,4]{0,2,1:T(4,128)S(1)}, f32[16,8,4,128]{3,0,2,1:T(8,128)S(1)}, pred[4,1,256]{2,1,0:T(4,12...) while((s32[]{:T(128)}, f32[16,8,4]{0,2,1:T(4,128)S(1)}, ...), condition=%wide.region_8.9_spmd, body=%wide.region_5.8_spmd.sunk | while | flops 68420608 | bytes 7505253 | solution.py:58
  157.9 1.3 constant_dynamic-slice_fusion.3
  160.7 1.3 constant_dynamic-slice_fusion.3
  167.0 1.5 reshape.208
  168.5 9.5 %all-to-all-start.2 = ((bf16[64,2,4096]{2,1,0:T(2,128)(2,1)}), bf16[64,2,4096]{2,1,0:T(2,128)(2,1)S(1)}, u32[]{:S(2)}, u32[]{:S(2)}) async-start(bf16[64,2,4096]{2,1,0:T(2,128)(2,1)} %reshape.208), calls=%async_computation.2 | async-start | bytes 2097152 | tf_op jit(solution)/shard_map/all_to_all | solution.py:150
  178.8 24.5 %all-to-all-done.2 = bf16[64,2,4096]{2,1,0:T(2,128)(2,1)S(1)} async-done(((bf16[64,2,4096]{2,1,0:T(2,128)(2,1)}), bf16[64,2,4096]{2,1,0:T(2,128)(2,1)S(1)}, u32[]{:S(2)}, u32[]{:S(2)}) %all-to-all-start.2) | async-done | bytes 1048608 | tf_op jit(solution)/shard_map/all_to_all | solution.py:150
  206.3 1.7 add_convert_fusion
  207.9 2.5 reshape.209
  210.5 6.8 %all-to-all-start.3 = ((bf16[64,2,4096]{2,1,0:T(2,128)(2,1)}), bf16[64,2,4096]{2,1,0:T(2,128)(2,1)}, u32[]{:S(2)}, u32[]{:S(2)}) async-start(bf16[64,2,4096]{2,1,0:T(2,128)(2,1)} %reshape.209), calls=%async_computation.3 | async-start | bytes 2097152 | tf_op jit(solution)/shard_map/all_to_all | solution.py:174
  217.4 2.4 multiply_convert_fusion
  219.8 2.3 convert_element_type.95
  223.1 2.8 fusion.13
  225.9 71.4 %all-reduce.3.cloned.1.call-done = (bf16[1,16,4096]{2,1,0:T(8,128)(2,1)}, bf16[1,16,4096]{2,1,0:T(8,128)(2,1)}) async-done(((bf16[1,16,4096]{2,1,0:T(8,128)(2,1)}, bf16[1,16,4096]{2,1,0:T(8,128)(2,1)}), (bf16[1,16,4096]{2,1,0:T(8,128)(2,1)}, bf16[1,16,4096]{2,1,0:T(8,128)(2,1)})) %all-reduce.3.cloned.1.call-update) | async-done | bytes 262160 | tf_op jit(solution)/shard_map/psum | solution.py:181
  297.3 1.6 broadcast_in_dim.108
  298.9 1.6 broadcast_in_dim.110
  300.5 1.5 reshape.210
  (97 shorter events, 17.7 us)
Async XLA Ops:
  7.2 197.9 %copy-start = (bf16[1,16,4096]{2,1,0:T(8,128)(2,1)S(1)}, bf16[1,16,4096]{2,1,0:T(8,128)(2,1)}, u32[]{:S(2)}) copy-start(bf16[1,16,4096]{2,1,0:T(8,128)(2,1)} %param.20) | copy-start | bytes 393220
  11.6 17.0 %copy-start.5 = (bf16[256,1024]{1,0:T(8,128)(2,1)S(1)}, bf16[256,1024]{1,0:T(8,128)(2,1)}, u32[]{:S(2)}) copy-start(bf16[256,1024]{1,0:T(8,128)(2,1)} %param.14) | copy-start | bytes 1572868
  11.6 18.5 %copy-start.7 = (bf16[16,4096]{1,0:T(8,128)(2,1)S(1)}, bf16[16,4096]{1,0:T(8,128)(2,1)}, u32[]{:S(2)}) copy-start(bf16[16,4096]{1,0:T(8,128)(2,1)} %param.12) | copy-start | bytes 393220
  11.6 18.6 %copy-start.4 = (bf16[256,1024]{1,0:T(8,128)(2,1)S(1)}, bf16[256,1024]{1,0:T(8,128)(2,1)}, u32[]{:S(2)}) copy-start(bf16[256,1024]{1,0:T(8,128)(2,1)} %param.13) | copy-start | bytes 1572868
  11.6 69.2 %all-to-all-start.1 = ((bf16[64,16,1024]{2,1,0:T(8,128)(2,1)}), bf16[64,16,1024]{2,1,0:T(8,128)(2,1)}, u32[]{:S(2)}, u32[]{:S(2)}) async-start(bf16[64,16,1024]{2,1,0:T(8,128)(2,1)} %stack.3), calls=%async_computation.1 | async-start | bytes 4194304 | tf_op jit(solution)/shard_map/all_to_all | solution.py:19
  28.5 2.7 copy-start.9
  28.5 2.8 copy-start.8
  28.5 126.7 %all-gather.2.cloned.1.call-start = ((), (), s32[]{:S(2)}) async-start(), calls=%async_computation.4 | async-start | bytes 2129920 | tf_op jit(solution)/shard_map/all_gather | solution.py:100
  80.8 87.6 %all-to-all-start = ((bf16[64,2,4096]{2,1,0:T(2,128)(2,1)}), bf16[64,2,4096]{2,1,0:T(2,128)(2,1)S(1)}, u32[]{:S(2)}, u32[]{:S(2)}) async-start(bf16[64,2,4096]{2,1,0:T(2,128)(2,1)} %reshape.199), calls=%async_computation | async-start | bytes 2097152 | tf_op jit(solution)/shard_map/all_to_all | solution.py:151
  168.5 10.0 %copy-start.6 = (bf16[1,16,4096]{2,1,0:T(8,128)(2,1)S(1)}, bf16[1,16,4096]{2,1,0:T(8,128)(2,1)}, u32[]{:S(2)}) copy-start(bf16[1,16,4096]{2,1,0:T(8,128)(2,1)} %param.21) | copy-start | bytes 393220
  168.5 34.9 %all-to-all-start.2 = ((bf16[64,2,4096]{2,1,0:T(2,128)(2,1)}), bf16[64,2,4096]{2,1,0:T(2,128)(2,1)S(1)}, u32[]{:S(2)}, u32[]{:S(2)}) async-start(bf16[64,2,4096]{2,1,0:T(2,128)(2,1)} %reshape.208), calls=%async_computation.2 | async-start | bytes 2097152 | tf_op jit(solution)/shard_map/all_to_all | solution.py:150
  178.4 26.1 %copy-start.1 = (bf16[128,4096]{1,0:T(8,128)(2,1)}, bf16[128,4096]{1,0:T(8,128)(2,1)S(1)}, u32[]{:S(2)}) copy-start(bf16[128,4096]{1,0:T(8,128)(2,1)S(1)} %reshape.200) | copy-start | bytes 3145732
  205.0 1.2 copy-start.2
  210.5 90.0 %all-to-all-start.3 = ((bf16[64,2,4096]{2,1,0:T(2,128)(2,1)}), bf16[64,2,4096]{2,1,0:T(2,128)(2,1)}, u32[]{:S(2)}, u32[]{:S(2)}) async-start(bf16[64,2,4096]{2,1,0:T(2,128)(2,1)} %reshape.209), calls=%async_computation.3 | async-start | bytes 2097152 | tf_op jit(solution)/shard_map/all_to_all | solution.py:174
  217.3 79.9 %all-reduce.3.cloned.1.call-start = ((), (), s32[]{:S(2)}) async-start(), calls=%async_computation.5 | async-start | bytes 524288 | tf_op jit(solution)/shard_map/psum | solution.py:181
  219.8 3.3 %copy-start.3 = (bf16[128,4096]{1,0:T(8,128)(2,1)S(1)}, bf16[128,4096]{1,0:T(8,128)(2,1)}, u32[]{:S(2)}) copy-start(bf16[128,4096]{1,0:T(8,128)(2,1)} %copy-done.1) | copy-start | bytes 3145732
Sparse Core Ops, SparseCore 0:
  32.9 122.1 all-gather.1
  226.0 71.1 all-reduce.2
